TPU v7x, 256 devices: a whole 4x4x8 slice. The times are simulated.
256 devices in a mesh: row: 64 (over z, y, core), col: 4 (over x).
Axes of the slice: x: 4, y: 4, z: 8, core: 2. Of those that a mesh axis runs over, the one named last changes fastest.
Arguments:
- train_points: float32 [16, 3, 64, 128], P(None, None, 'row'), may hold values from -6 to 6
- new_points: float32 [16, 256], replicated, may hold values from -6 to 6
- lengthscales: float32 [16], replicated, may hold values from 2.5 to 6
- factor: float32 [3, 64, 128, 3, 4, 2048], P(None, 'row', None, None, 'col'), may hold values from -0.02734375 to 0.02734375
- diag_inverse: float32 [3, 64, 128, 4, 2048], P(None, 'row', None, 'col'), may hold values from -3 to 3
Outputs:
- solution: float32 [3, 4, 64, 32, 256], P(None, 'col', 'row')
All inputs are finite; a program needn't handle non-finite values.
Results may differ from a plain program's by a relative error of at most 0.0001.
Values sent between devices are 32-bit elements; how exact they have to be, the bound alone decides.
No kernel may reach another device: no remote copies, remote signals or barrier semaphores. Data moves between devices by JAX's collectives and lax.ppermute only.
A program may use at most 128 MiB of HBM per device.

v0:
```python
import jax
import jax.numpy as jnp
from jax import lax
from jax.sharding import PartitionSpec as P


def on_device(train_points, new_points, lengthscales, factor, diag_inverse):
    highest = lax.Precision.HIGHEST
    panels = factor.shape[0]
    block_rows = factor.shape[2]
    quarter_cols = factor.shape[5]
    new_count = new_points.shape[1]
    share_rows = block_rows // lax.axis_size("col")
    scaled_train = (train_points / lengthscales[:, None, None, None]).reshape(
        train_points.shape[0], panels * block_rows
    )
    scaled_new = new_points / lengthscales[:, None]
    inner_products = jnp.dot(scaled_train.T, scaled_new, precision=highest)
    sqdist = (
        jnp.sum(scaled_train * scaled_train, axis=0)[:, None]
        + jnp.sum(scaled_new * scaled_new, axis=0)[None, :]
        - 2.0 * inner_products
    )
    kernel = jnp.exp(-0.5 * sqdist).reshape(panels, block_rows, new_count)
    factor_blocks = factor.reshape(panels, block_rows, panels, quarter_cols)
    inverse_blocks = diag_inverse.reshape(panels, block_rows, quarter_cols)
    panel_numbers = jnp.arange(panels)

    def update(partial_rows, panel, quarter, after):
        column_slab = lax.dynamic_index_in_dim(factor_blocks, panel, axis=2, keepdims=False)
        change = jnp.einsum("piq,qm->pim", column_slab, quarter, precision=highest)
        below = (panel_numbers > after)[:, None, None]
        return partial_rows + jnp.where(below, change, 0.0)

    def advance(panel, loop_state):
        partial_rows, solved, pending = loop_state
        own_partial = lax.dynamic_index_in_dim(partial_rows, panel, 0, keepdims=False)
        summed = lax.psum(own_partial, "col")
        residual = lax.dynamic_index_in_dim(kernel, panel, 0, keepdims=False) - summed
        inverse_block = lax.dynamic_index_in_dim(inverse_blocks, panel, 0, keepdims=False)
        product = jnp.einsum("iq,im->qm", inverse_block, residual, precision=highest)
        own_rows = lax.psum_scatter(product, "row", scatter_dimension=0, tiled=True)
        quarter = lax.all_gather(own_rows, "row", axis=0, tiled=True)
        solved = lax.dynamic_update_index_in_dim(solved, own_rows, panel, 0)
        partial_rows = update(partial_rows, panel, quarter, panel)
        return (partial_rows, solved, pending)

    initial = (
        jnp.zeros((panels, block_rows, new_count), jnp.float32),
        jnp.zeros((panels, share_rows, new_count), jnp.float32),
        jnp.zeros((quarter_cols, new_count), jnp.float32),
    )
    partial_rows, solved, pending = lax.fori_loop(0, panels, advance, initial)
    return solved.reshape(panels, 1, 1, share_rows, new_count)


def solution(mesh):
    return jax.shard_map(
        on_device,
        mesh=mesh,
        in_specs=(
            P(None, None, "row", None),
            P(),
            P(),
            P(None, "row", None, None, "col", None),
            P(None, "row", None, "col", None),
        ),
        out_specs=P(None, "col", "row", None, None),
        check_vma=False,
    )
```

profile of v0, /device:TPU:1, one launch (start us, length us, event | category | flops | bytes accessed | tf_op | source)
XLA Modules:
  0.0 868.2 jit_solution(1024487664733539460)
XLA Ops:
  6.5 0.9 fusion.27
  7.4 0.8 multiply_reduce_fusion.1
  8.3 2.0 fusion.24
  10.3 12.1 %copy.15 = f32[3,1,128,3,1,2048]{5,2,0,3,4,1:T(8,128)} copy(f32[3,1,128,3,1,2048]{5,4,3,2,1,0:T(1,128)} %param.10) | data formatting | bytes 18874368 | tf_op args[3]
  22.4 1.4 copy.16
  23.8 837.8 %while.16 = (s32[]{:T(128)}, f32[3,128,256]{2,1,0:T(8,128)}, f32[3,32,256]{2,1,0:T(8,128)}, f32[3,128,3,2048]{3,1,0,2:T(8,128)}, f32[3,128,2048]{2,1,0:T(8,128)S...) while((s32[]{:T(128)}, f32[3,128,256]{2,1,0:T(8,128)}, f32[3,32,256]{2,1,0:T(8,128)}, ...), condition=%wide.region_5.6_spmd.clone, body=%wide.region_2.5_spmd.clone.sunk | while | flops 3221585920 | bytes 24118516 | solution.py:53
  24.1 0.7 dynamic-slice_bitcast_fusion.2
  24.9 50.3 %all-reduce.2.cloned.1.call-done = f32[128,256]{1,0:T(8,128)} async-done(((f32[128,256]{1,0:T(8,128)}), f32[128,256]{1,0:T(8,128)}) %all-reduce.2.cloned.1.call-update) | async-done | bytes 131088 | tf_op jit(solution)/shard_map/while/body/eval_jaxpr/psum | solution.py:38
  75.2 4.1 fusion.36
  79.3 0.0 all-gather.2.cloned.1.call-start
  79.4 138.6 %reduce-scatter.2.cloned.1.call-done = f32[32,256]{1,0:T(8,128)} async-done(((f32[2048,256]{1,0:T(8,128)}), f32[32,256]{1,0:T(8,128)}) %reduce-scatter.2.cloned.1.call-update) | async-done | bytes 32784 | tf_op jit(solution)/shard_map/while/body/eval_jaxpr/reduce_scatter | solution.py:42
  218.1 1.4 bitcast_dynamic-update-slice_fusion.2
  219.4 82.4 %all-gather.2.cloned.1.call-done = f32[2048,256]{1,0:T(8,128)} async-done(((f32[32,256]{1,0:T(8,128)}), f32[2048,256]{1,0:T(8,128)}) %all-gather.2.cloned.1.call-update) | async-done | bytes 2097168 | tf_op jit(solution)/shard_map/while/body/eval_jaxpr/all_gather | solution.py:43
  301.9 6.0 fusion.37
  307.8 1.0 broadcast_select_fusion.2
  308.9 0.7 dynamic-slice_bitcast_fusion.2
  309.6 42.5 %all-reduce.2.cloned.1.call-done = f32[128,256]{1,0:T(8,128)} async-done(((f32[128,256]{1,0:T(8,128)}), f32[128,256]{1,0:T(8,128)}) %all-reduce.2.cloned.1.call-update) | async-done | bytes 131088 | tf_op jit(solution)/shard_map/while/body/eval_jaxpr/psum | solution.py:38
  352.1 4.1 fusion.36
  356.2 0.0 all-gather.2.cloned.1.call-start
  356.3 138.2 %reduce-scatter.2.cloned.1.call-done = f32[32,256]{1,0:T(8,128)} async-done(((f32[2048,256]{1,0:T(8,128)}), f32[32,256]{1,0:T(8,128)}) %reduce-scatter.2.cloned.1.call-update) | async-done | bytes 32784 | tf_op jit(solution)/shard_map/while/body/eval_jaxpr/reduce_scatter | solution.py:42
  494.5 1.4 bitcast_dynamic-update-slice_fusion.2
  495.9 82.6 %all-gather.2.cloned.1.call-done = f32[2048,256]{1,0:T(8,128)} async-done(((f32[32,256]{1,0:T(8,128)}), f32[2048,256]{1,0:T(8,128)}) %all-gather.2.cloned.1.call-update) | async-done | bytes 2097168 | tf_op jit(solution)/shard_map/while/body/eval_jaxpr/all_gather | solution.py:43
  578.5 6.0 fusion.37
  584.5 1.0 broadcast_select_fusion.2
  585.5 0.7 dynamic-slice_bitcast_fusion.2
  586.2 42.8 %all-reduce.2.cloned.1.call-done = f32[128,256]{1,0:T(8,128)} async-done(((f32[128,256]{1,0:T(8,128)}), f32[128,256]{1,0:T(8,128)}) %all-reduce.2.cloned.1.call-update) | async-done | bytes 131088 | tf_op jit(solution)/shard_map/while/body/eval_jaxpr/psum | solution.py:38
  629.0 4.1 fusion.36
  633.2 0.0 all-gather.2.cloned.1.call-start
  633.2 138.6 %reduce-scatter.2.cloned.1.call-done = f32[32,256]{1,0:T(8,128)} async-done(((f32[2048,256]{1,0:T(8,128)}), f32[32,256]{1,0:T(8,128)}) %reduce-scatter.2.cloned.1.call-update) | async-done | bytes 32784 | tf_op jit(solution)/shard_map/while/body/eval_jaxpr/reduce_scatter | solution.py:42
  771.9 1.4 bitcast_dynamic-update-slice_fusion.2
  773.3 82.4 %all-gather.2.cloned.1.call-done = f32[2048,256]{1,0:T(8,128)} async-done(((f32[32,256]{1,0:T(8,128)}), f32[2048,256]{1,0:T(8,128)}) %all-gather.2.cloned.1.call-update) | async-done | bytes 2097168 | tf_op jit(solution)/shard_map/while/body/eval_jaxpr/all_gather | solution.py:43
  855.7 6.0 fusion.37
  (23 shorter events, 0.4 us)
Async XLA Ops:
  10.3 12.1 %copy-start = (f32[3,1,128,1,2048]{4,3,2,1,0:T(1,128)S(1)}, f32[3,1,128,1,2048]{4,3,2,1,0:T(1,128)}, u32[]{:S(2)}) copy-start(f32[3,1,128,1,2048]{4,3,2,1,0:T(1,128)} %param.11) | copy-start | bytes 9437188
  24.0 51.2 %all-reduce.2.cloned.1.call-start = ((), (), s32[]{:S(2)}) async-start(), calls=%async_computation.1 | async-start | bytes 262144 | tf_op jit(solution)/shard_map/while/body/eval_jaxpr/psum | solution.py:38
  24.8 193.2 %reduce-scatter.2.cloned.1.call-start = ((), (), s32[]{:S(2)}) async-start(), calls=%async_computation.2 | async-start | bytes 2129920 | tf_op jit(solution)/shard_map/while/body/eval_jaxpr/reduce_scatter | solution.py:42
  79.3 222.5 %all-gather.2.cloned.1.call-start = ((), (), s32[]{:S(2)}) async-start(), calls=%async_computation.3 | async-start | bytes 2129920 | tf_op jit(solution)/shard_map/while/body/eval_jaxpr/all_gather | solution.py:43
  307.8 44.3 %all-reduce.2.cloned.1.call-start = ((), (), s32[]{:S(2)}) async-start(), calls=%async_computation.1 | async-start | bytes 262144 | tf_op jit(solution)/shard_map/while/body/eval_jaxpr/psum | solution.py:38
  309.6 184.9 %reduce-scatter.2.cloned.1.call-start = ((), (), s32[]{:S(2)}) async-start(), calls=%async_computation.2 | async-start | bytes 2129920 | tf_op jit(solution)/shard_map/while/body/eval_jaxpr/reduce_scatter | solution.py:42
  356.2 222.2 %all-gather.2.cloned.1.call-start = ((), (), s32[]{:S(2)}) async-start(), calls=%async_computation.3 | async-start | bytes 2129920 | tf_op jit(solution)/shard_map/while/body/eval_jaxpr/all_gather | solution.py:43
  584.4 44.6 %all-reduce.2.cloned.1.call-start = ((), (), s32[]{:S(2)}) async-start(), calls=%async_computation.1 | async-start | bytes 262144 | tf_op jit(solution)/shard_map/while/body/eval_jaxpr/psum | solution.py:38
  586.2 185.7 %reduce-scatter.2.cloned.1.call-start = ((), (), s32[]{:S(2)}) async-start(), calls=%async_computation.2 | async-start | bytes 2129920 | tf_op jit(solution)/shard_map/while/body/eval_jaxpr/reduce_scatter | solution.py:42
  633.2 222.5 %all-gather.2.cloned.1.call-start = ((), (), s32[]{:S(2)}) async-start(), calls=%async_computation.3 | async-start | bytes 2129920 | tf_op jit(solution)/shard_map/while/body/eval_jaxpr/all_gather | solution.py:43
Sparse Core Ops, SparseCore 0:
  27.2 47.9 all-reduce.1
  79.8 138.1 reduce-scatter.1
  220.8 81.0 all-gather.1
  310.7 41.4 all-reduce.1
  356.6 137.9 reduce-scatter.1
  497.1 81.3 all-gather.1
  587.6 41.4 all-reduce.1
  633.6 138.1 reduce-scatter.1
  774.6 81.0 all-gather.1
where the time goes:
time: 869 us; the launch traced here: 868 us
  waiting for transfers between devices  799 us (92%)
  matrix products  32.3 us (4%)
  local copies, waits for them, and re-layouts  19.7 us (2%)
  between operations  13.1 us (2%)
    reduce_scatter x3, waiting for transfers between devices, advance(): own_rows = lax.psum_scatter(product, 'row', scatter_dimension=0, tiled=True)  415 us
    all_gather x3, waiting for transfers between devices, advance(): quarter = lax.all_gather(own_rows, 'row', axis=0, tiled=True)  247 us
    psum x3, waiting for transfers between devices, advance(): summed = lax.psum(own_partial, 'col')  136 us
    dot_general x3, matrix products, update(): change = jnp.einsum('piq,qm->pim', column_slab, quarter, precision=highest)  17.9 us
  transfers between devices with their start and end apart: 9, of which 9 were waited for; matrix products, arithmetic and copies ran while one was open for 0% of the time, Pallas kernels for 0%

commit v1 on v0

--- a/solution.py
+++ b/solution.py
@@ -40,7 +40,8 @@
         inverse_block = lax.dynamic_index_in_dim(inverse_blocks, panel, 0, keepdims=False)
         product = jnp.einsum("iq,im->qm", inverse_block, residual, precision=highest)
         own_rows = lax.psum_scatter(product, "row", scatter_dimension=0, tiled=True)
-        quarter = lax.all_gather(own_rows, "row", axis=0, tiled=True)
+        repeated = jnp.stack([own_rows] * lax.axis_size("row"))
+        quarter = jnp.concatenate(lax.all_to_all(repeated, "row", 0, 0), axis=0)
         solved = lax.dynamic_update_index_in_dim(solved, own_rows, panel, 0)
         partial_rows = update(partial_rows, panel, quarter, panel)
         return (partial_rows, solved, pending)

time: 869 us -> 812 us (0.934)
  waiting for transfers between devices: 799 us -> 700 us
  starting transfers between devices: 0.3 us -> 39.1 us
    all_gather x3 -> x0, waiting for transfers between devices: 247 us -> none  [advance(): quarter = lax.all_gather(own_rows, 'row', axis=0, tiled=True)]
    all_to_all x0 -> x3, waiting for transfers between devices: none -> 147 us  [advance(): quarter = jnp.concatenate(lax.all_to_all(repeated, 'row', 0, 0), axis=0)]
    all_to_all x0 -> x3, starting transfers between devices: none -> 38.9 us  [advance(): quarter = jnp.concatenate(lax.all_to_all(repeated, 'row', 0, 0), axis=0)]
where the time goes in v1:
time: 812 us; the launch traced here: 811 us
  waiting for transfers between devices  700 us (86%)
  starting transfers between devices  39.1 us (5%)
  matrix products  28.2 us (3%)
  local copies, waits for them, and re-layouts  28.1 us (3%)
  between operations  13.4 us (2%)
    reduce_scatter x3, waiting for transfers between devices, advance(): own_rows = lax.psum_scatter(product, 'row', scatter_dimension=0, tiled=True)  414 us
    all_to_all x3, waiting for transfers between devices, advance(): quarter = jnp.concatenate(lax.all_to_all(repeated, 'row', 0, 0), axis=0)  147 us
    psum x3, waiting for transfers between devices, advance(): summed = lax.psum(own_partial, 'col')  138 us
    all_to_all x3, starting transfers between devices, advance(): quarter = jnp.concatenate(lax.all_to_all(repeated, 'row', 0, 0), axis=0)  38.9 us
    unnamed x2, local copies, waits for them, and re-layouts  16.9 us
  transfers between devices with their start and end apart: 9, of which 9 were waited for; matrix products, arithmetic and copies ran while one was open for 0% of the time, Pallas kernels for 0%

profile of v1, /device:TPU:1, one launch (start us, length us, event | category | flops | bytes accessed | tf_op | source)
XLA Modules:
  0.0 810.9 jit_solution(12055433137899751203)
XLA Ops:
  6.5 0.8 multiply_reduce_fusion.1
  7.3 0.9 fusion.22
  8.3 1.3 fusion.19
  9.6 4.9 copy.16
  14.5 12.0 %copy.15 = f32[3,1,128,3,1,2048]{5,2,0,3,4,1:T(8,128)} copy(f32[3,1,128,3,1,2048]{5,4,3,2,1,0:T(1,128)} %param.10) | data formatting | bytes 18874368 | tf_op args[3]
  26.4 777.6 %while.16 = (s32[]{:T(128)}, f32[3,128,256]{2,1,0:T(8,128)S(1)}, f32[3,32,256]{2,1,0:T(8,128)}, f32[3,128,3,2048]{3,1,0,2:T(8,128)}, f32[3,128,2048]{2,1,0:T(8,1...) while((s32[]{:T(128)}, f32[3,128,256]{2,1,0:T(8,128)S(1)}, f32[3,32,256]{2,1,0:T(8,128)}, ...), condition=%wide.region_5.6_spmd.clone, body=%wide.region_2.5_spmd.clone.sunk | while | flops 3221585920 | bytes 26281224 | solution.py:54
  26.5 0.7 dynamic-slice_bitcast_fusion.2
  27.2 50.4 %all-reduce.2.cloned.1.call-done = f32[128,256]{1,0:T(8,128)} async-done(((f32[128,256]{1,0:T(8,128)}), f32[128,256]{1,0:T(8,128)}) %all-reduce.2.cloned.1.call-update) | async-done | bytes 131088 | tf_op jit(solution)/shard_map/while/body/eval_jaxpr/psum | solution.py:38
  77.6 4.4 fusion.32
  82.0 138.4 %reduce-scatter.2.cloned.1.call-done = f32[32,256]{1,0:T(8,128)} async-done(((f32[2048,256]{1,0:T(8,128)}), f32[32,256]{1,0:T(8,128)}) %reduce-scatter.2.cloned.1.call-update) | async-done | bytes 32784 | tf_op jit(solution)/shard_map/while/body/eval_jaxpr/reduce_scatter | solution.py:42
  220.4 2.4 stack.13
  222.9 12.7 %all-to-all-start = ((f32[64,32,256]{2,1,0:T(8,128)}), f32[64,32,256]{2,1,0:T(8,128)S(1)}, u32[]{:S(2)}, u32[]{:S(2)}) async-start(f32[64,32,256]{2,1,0:T(8,128)} %stack.13), calls=%async_computation.1 | async-start | bytes 4194304 | tf_op jit(solution)/shard_map/while/body/eval_jaxpr/all_to_all | solution.py:44
  235.6 0.6 bitcast_dynamic-update-slice_fusion.2
  236.2 49.0 %all-to-all-done = f32[64,32,256]{2,1,0:T(8,128)S(1)} async-done(((f32[64,32,256]{2,1,0:T(8,128)}), f32[64,32,256]{2,1,0:T(8,128)S(1)}, u32[]{:S(2)}, u32[]{:S(2)}) %all-to-all-start) | async-done | bytes 2097184 | tf_op jit(solution)/shard_map/while/body/eval_jaxpr/all_to_all | solution.py:44
  285.3 4.5 fusion.33
  289.9 0.7 dynamic-slice_bitcast_fusion.2
  290.7 44.1 %all-reduce.2.cloned.1.call-done = f32[128,256]{1,0:T(8,128)} async-done(((f32[128,256]{1,0:T(8,128)}), f32[128,256]{1,0:T(8,128)}) %all-reduce.2.cloned.1.call-update) | async-done | bytes 131088 | tf_op jit(solution)/shard_map/while/body/eval_jaxpr/psum | solution.py:38
  334.8 4.4 fusion.32
  339.3 138.1 %reduce-scatter.2.cloned.1.call-done = f32[32,256]{1,0:T(8,128)} async-done(((f32[2048,256]{1,0:T(8,128)}), f32[32,256]{1,0:T(8,128)}) %reduce-scatter.2.cloned.1.call-update) | async-done | bytes 32784 | tf_op jit(solution)/shard_map/while/body/eval_jaxpr/reduce_scatter | solution.py:42
  477.3 2.4 stack.13
  479.8 13.0 %all-to-all-start = ((f32[64,32,256]{2,1,0:T(8,128)}), f32[64,32,256]{2,1,0:T(8,128)S(1)}, u32[]{:S(2)}, u32[]{:S(2)}) async-start(f32[64,32,256]{2,1,0:T(8,128)} %stack.13), calls=%async_computation.1 | async-start | bytes 4194304 | tf_op jit(solution)/shard_map/while/body/eval_jaxpr/all_to_all | solution.py:44
  492.8 0.6 bitcast_dynamic-update-slice_fusion.2
  493.4 49.0 %all-to-all-done = f32[64,32,256]{2,1,0:T(8,128)S(1)} async-done(((f32[64,32,256]{2,1,0:T(8,128)}), f32[64,32,256]{2,1,0:T(8,128)S(1)}, u32[]{:S(2)}, u32[]{:S(2)}) %all-to-all-start) | async-done | bytes 2097184 | tf_op jit(solution)/shard_map/while/body/eval_jaxpr/all_to_all | solution.py:44
  542.5 4.5 fusion.33
  547.1 0.7 dynamic-slice_bitcast_fusion.2
  547.9 43.8 %all-reduce.2.cloned.1.call-done = f32[128,256]{1,0:T(8,128)} async-done(((f32[128,256]{1,0:T(8,128)}), f32[128,256]{1,0:T(8,128)}) %all-reduce.2.cloned.1.call-update) | async-done | bytes 131088 | tf_op jit(solution)/shard_map/while/body/eval_jaxpr/psum | solution.py:38
  591.7 4.4 fusion.32
  596.2 138.0 %reduce-scatter.2.cloned.1.call-done = f32[32,256]{1,0:T(8,128)} async-done(((f32[2048,256]{1,0:T(8,128)}), f32[32,256]{1,0:T(8,128)}) %reduce-scatter.2.cloned.1.call-update) | async-done | bytes 32784 | tf_op jit(solution)/shard_map/while/body/eval_jaxpr/reduce_scatter | solution.py:42
  734.2 2.4 stack.13
  736.7 13.1 %all-to-all-start = ((f32[64,32,256]{2,1,0:T(8,128)}), f32[64,32,256]{2,1,0:T(8,128)S(1)}, u32[]{:S(2)}, u32[]{:S(2)}) async-start(f32[64,32,256]{2,1,0:T(8,128)} %stack.13), calls=%async_computation.1 | async-start | bytes 4194304 | tf_op jit(solution)/shard_map/while/body/eval_jaxpr/all_to_all | solution.py:44
  750.4 49.0 %all-to-all-done = f32[64,32,256]{2,1,0:T(8,128)S(1)} async-done(((f32[64,32,256]{2,1,0:T(8,128)}), f32[64,32,256]{2,1,0:T(8,128)S(1)}, u32[]{:S(2)}, u32[]{:S(2)}) %all-to-all-start) | async-done | bytes 2097184 | tf_op jit(solution)/shard_map/while/body/eval_jaxpr/all_to_all | solution.py:44
  799.5 4.5 fusion.33
  (27 shorter events, 1.1 us)
Async XLA Ops:
  26.4 51.1 %all-reduce.2.cloned.1.call-start = ((), (), s32[]{:S(2)}) async-start(), calls=%async_computation.2 | async-start | bytes 262144 | tf_op jit(solution)/shard_map/while/body/eval_jaxpr/psum | solution.py:38
  27.2 193.2 %reduce-scatter.2.cloned.1.call-start = ((), (), s32[]{:S(2)}) async-start(), calls=%async_computation.3 | async-start | bytes 2129920 | tf_op jit(solution)/shard_map/while/body/eval_jaxpr/reduce_scatter | solution.py:42
  220.4 15.2 %copy-start = (f32[32,256]{1,0:T(8,128)S(1)}, f32[32,256]{1,0:T(8,128)}, u32[]{:S(2)}) copy-start(f32[32,256]{1,0:T(8,128)} %reduce-scatter.2.cloned.1.call-done) | copy-start | bytes 98308 | tf_op jit(solution)/shard_map/while
  222.9 62.4 %all-to-all-start = ((f32[64,32,256]{2,1,0:T(8,128)}), f32[64,32,256]{2,1,0:T(8,128)S(1)}, u32[]{:S(2)}, u32[]{:S(2)}) async-start(f32[64,32,256]{2,1,0:T(8,128)} %stack.13), calls=%async_computation.1 | async-start | bytes 4194304 | tf_op jit(solution)/shard_map/while/body/eval_jaxpr/all_to_all | solution.py:44
  289.8 45.0 %all-reduce.2.cloned.1.call-start = ((), (), s32[]{:S(2)}) async-start(), calls=%async_computation.2 | async-start | bytes 262144 | tf_op jit(solution)/shard_map/while/body/eval_jaxpr/psum | solution.py:38
  290.6 186.7 %reduce-scatter.2.cloned.1.call-start = ((), (), s32[]{:S(2)}) async-start(), calls=%async_computation.3 | async-start | bytes 2129920 | tf_op jit(solution)/shard_map/while/body/eval_jaxpr/reduce_scatter | solution.py:42
  477.3 15.5 %copy-start = (f32[32,256]{1,0:T(8,128)S(1)}, f32[32,256]{1,0:T(8,128)}, u32[]{:S(2)}) copy-start(f32[32,256]{1,0:T(8,128)} %reduce-scatter.2.cloned.1.call-done) | copy-start | bytes 98308 | tf_op jit(solution)/shard_map/while
  479.8 62.7 %all-to-all-start = ((f32[64,32,256]{2,1,0:T(8,128)}), f32[64,32,256]{2,1,0:T(8,128)S(1)}, u32[]{:S(2)}, u32[]{:S(2)}) async-start(f32[64,32,256]{2,1,0:T(8,128)} %stack.13), calls=%async_computation.1 | async-start | bytes 4194304 | tf_op jit(solution)/shard_map/while/body/eval_jaxpr/all_to_all | solution.py:44
  547.0 44.7 %all-reduce.2.cloned.1.call-start = ((), (), s32[]{:S(2)}) async-start(), calls=%async_computation.2 | async-start | bytes 262144 | tf_op jit(solution)/shard_map/while/body/eval_jaxpr/psum | solution.py:38
  547.8 186.4 %reduce-scatter.2.cloned.1.call-start = ((), (), s32[]{:S(2)}) async-start(), calls=%async_computation.3 | async-start | bytes 2129920 | tf_op jit(solution)/shard_map/while/body/eval_jaxpr/reduce_scatter | solution.py:42
  734.2 15.6 %copy-start = (f32[32,256]{1,0:T(8,128)S(1)}, f32[32,256]{1,0:T(8,128)}, u32[]{:S(2)}) copy-start(f32[32,256]{1,0:T(8,128)} %reduce-scatter.2.cloned.1.call-done) | copy-start | bytes 98308 | tf_op jit(solution)/shard_map/while
  736.7 62.8 %all-to-all-start = ((f32[64,32,256]{2,1,0:T(8,128)}), f32[64,32,256]{2,1,0:T(8,128)S(1)}, u32[]{:S(2)}, u32[]{:S(2)}) async-start(f32[64,32,256]{2,1,0:T(8,128)} %stack.13), calls=%async_computation.1 | async-start | bytes 4194304 | tf_op jit(solution)/shard_map/while/body/eval_jaxpr/all_to_all | solution.py:44
Sparse Core Ops, SparseCore 0:
  29.6 47.9 all-reduce.1
  82.2 138.1 reduce-scatter.1
  293.0 41.7 all-reduce.1
  339.4 137.9 reduce-scatter.1
  549.9 41.7 all-reduce.1
  596.3 137.8 reduce-scatter.1
